TPU v7x, 32 devices: a whole 2x2x4 slice. The times are simulated.
32 devices in a mesh: fsdp: 4 (over y, x), ctx: 4 (over z), tp: 2 (over core).
Axes of the slice: x: 2, y: 2, z: 4, core: 2. Of those that a mesh axis runs over, the one named last changes fastest.
Arguments:
- image_input: bfloat16 [4, 2048, 768], P('fsdp', 'ctx'), may hold values from -6 to 6
- image_segments: int32 [4, 2048], P('fsdp'), may hold values from 0 to 5, never falling along the last dimension, each value on 1 to 1536 neighbouring positions
- image_cotangent: bfloat16 [4, 2048, 768], P('fsdp', 'ctx'), may hold values from -6 to 6
- image_gains: bfloat16 [2, 768], P(None, 'fsdp'), may hold values from 0.099609375 to 1.8984375
- image_shifts: bfloat16 [4, 768], P(None, 'fsdp'), may hold values from -3 to 3
- image_head_bias: bfloat16 [2, 2304], P('tp', 'fsdp'), may hold values from -3 to 3
- image_qkv_weight: bfloat16 [3, 768, 768], P(None, 'fsdp', 'tp'), may hold values from -0.21875 to 0.21875
- image_proj_weight: bfloat16 [768, 768], P('tp', 'fsdp'), may hold values from -0.875 to 0.875
- image_up_weight: bfloat16 [768, 3072], P('fsdp', 'tp'), may hold values from -0.21875 to 0.21875
- image_down_weight: bfloat16 [3072, 768], P('tp', 'fsdp'), may hold values from -0.109375 to 0.109375
- text_input: bfloat16 [4, 2048, 512], P('fsdp', 'ctx'), may hold values from -6 to 6
- text_segments: int32 [4, 2048], P('fsdp'), may hold values from 0 to 5, never falling along the last dimension, each value on 1 to 1536 neighbouring positions
- text_cotangent: bfloat16 [4, 2048, 512], P('fsdp', 'ctx'), may hold values from -6 to 6
- text_gains: bfloat16 [2, 512], P(None, 'fsdp'), may hold values from 0.099609375 to 1.8984375
- text_shifts: bfloat16 [4, 512], P(None, 'fsdp'), may hold values from -3 to 3
- text_head_bias: bfloat16 [2, 1536], P('tp', 'fsdp'), may hold values from -3 to 3
- text_qkv_weight: bfloat16 [3, 512, 512], P(None, 'fsdp', 'tp'), may hold values from -0.25 to 0.25
- text_proj_weight: bfloat16 [512, 512], P('tp', 'fsdp'), may hold values from -1 to 1
- text_up_weight: bfloat16 [512, 2048], P('fsdp', 'tp'), may hold values from -0.25 to 0.25
- text_down_weight: bfloat16 [2048, 512], P('tp', 'fsdp'), may hold values from -0.125 to 0.125
Outputs:
- image_output: bfloat16 [4, 2048, 768], P('fsdp', 'ctx')
- image_input_grad: float32 [4, 2048, 768], P('fsdp', 'ctx')
- image_gains_grad: float32 [2, 768], P(None, 'fsdp')
- image_shifts_grad: float32 [4, 768], P(None, 'fsdp')
- image_head_bias_grad: float32 [2, 2304], P('tp', 'fsdp')
- image_qkv_grad: float32 [3, 768, 768], P(None, 'fsdp', 'tp')
- image_proj_grad: float32 [768, 768], P('tp', 'fsdp')
- image_up_grad: float32 [768, 3072], P('fsdp', 'tp')
- image_down_grad: float32 [3072, 768], P('tp', 'fsdp')
- text_output: bfloat16 [4, 2048, 512], P('fsdp', 'ctx')
- text_input_grad: float32 [4, 2048, 512], P('fsdp', 'ctx')
- text_gains_grad: float32 [2, 512], P(None, 'fsdp')
- text_shifts_grad: float32 [4, 512], P(None, 'fsdp')
- text_head_bias_grad: float32 [2, 1536], P('tp', 'fsdp')
- text_qkv_grad: float32 [3, 512, 512], P(None, 'fsdp', 'tp')
- text_proj_grad: float32 [512, 512], P('tp', 'fsdp')
- text_up_grad: float32 [512, 2048], P('fsdp', 'tp')
- text_down_grad: float32 [2048, 512], P('tp', 'fsdp')
Inputs may be any that keep to these rules, and one draw needn't show every extreme that they name: `image_segments`: along each sequence segment numbers never fall; every document has 1 to 1536 tokens, and one has exactly that many. `text_segments`: along each sequence segment numbers never fall; every document has 1 to 1536 tokens, and one has exactly that many.
All inputs are finite; a program needn't handle non-finite values.
Results may differ from a plain program's by a relative error of at most 0.012.
Values may be sent and summed in bfloat16 or wider, within the bound.
A program may use at most 128 MiB of HBM per device.

v0:
```python
import jax
import jax.numpy as jnp
from jax import lax
from jax.sharding import PartitionSpec as P

HD = 64


def layer_stats(rows):
    row_mean = jnp.mean(rows, axis=-1, keepdims=True)
    centred = rows - row_mean
    inv_std = lax.rsqrt(jnp.mean(centred * centred, axis=-1, keepdims=True) + 1e-05)
    return (centred * inv_std, inv_std)


def norm_back(grad_normed_out, normed, inv_std, gain):
    scaled = grad_normed_out * gain
    return inv_std * (
        scaled
        - jnp.mean(scaled, axis=-1, keepdims=True)
        - normed * jnp.mean(scaled * normed, axis=-1, keepdims=True)
    )


def tensor_sum(partial_rows):
    return lax.psum(partial_rows, "tp")


def run_block(
    rows_in,
    seg_row,
    cotangent,
    gains,
    shifts,
    head_bias,
    qkv_weight,
    proj_weight,
    up_weight,
    down_weight,
    causal,
):
    gain_full, shift_full, bias_full, qkv_full, proj_full, up_full, down_full = (
        lax.all_gather(gains, "fsdp", axis=1, tiled=True),
        lax.all_gather(shifts, "fsdp", axis=1, tiled=True),
        lax.all_gather(head_bias, "fsdp", axis=1, tiled=True),
        lax.all_gather(qkv_weight, "fsdp", axis=1, tiled=True),
        lax.all_gather(proj_weight, "fsdp", axis=1, tiled=True),
        lax.all_gather(up_weight, "fsdp", axis=0, tiled=True),
        lax.all_gather(down_weight, "fsdp", axis=1, tiled=True),
    )
    gain_vals = gain_full.astype(jnp.float32)
    shift_vals = shift_full.astype(jnp.float32)
    bias_vals = bias_full[0].astype(jnp.float32)
    tp_width = qkv_full.shape[2]
    local_rows = rows_in.shape[1]
    seq_length = seg_row.shape[1]
    head_local = tp_width // HD
    rows = rows_in[0].astype(jnp.float32)
    row_start = lax.axis_index("ctx") * local_rows
    seg_all = seg_row[0]
    seg_query = lax.dynamic_slice_in_dim(seg_all, row_start, local_rows)
    query_pos = row_start + jnp.arange(local_rows, dtype=jnp.int32)
    key_pos = jnp.arange(seq_length, dtype=jnp.int32)
    allowed = seg_query[:, None] == seg_all[None, :]
    if causal:
        allowed = jnp.logical_and(allowed, key_pos[None, :] <= query_pos[:, None])

    def to_heads(matrix):
        return matrix.reshape(matrix.shape[0], head_local, HD).transpose(1, 0, 2)

    def from_heads(stacked):
        return stacked.transpose(1, 0, 2).reshape(stacked.shape[1], head_local * HD)

    normed_one, inv_one = layer_stats(rows)
    first_in = (normed_one * gain_vals[0] + shift_vals[0]).astype(jnp.bfloat16)
    queries = (
        jnp.dot(first_in, qkv_full[0], preferred_element_type=jnp.float32) + bias_vals[:tp_width]
    ).astype(jnp.bfloat16)
    key_rows = jnp.dot(first_in, qkv_full[1], preferred_element_type=jnp.float32).astype(
        jnp.bfloat16
    )
    values = (
        jnp.dot(first_in, qkv_full[2], preferred_element_type=jnp.float32)
        + bias_vals[tp_width : 2 * tp_width]
    ).astype(jnp.bfloat16)
    key_all, value_all = (
        lax.all_gather(key_rows, "ctx", axis=0, tiled=True),
        lax.all_gather(values, "ctx", axis=0, tiled=True),
    )
    query_heads = to_heads(queries)
    key_heads = to_heads(key_all)
    value_heads = to_heads(value_all)

    def attend(head_items):
        query_h, key_h, value_h = head_items
        scores = jnp.einsum("qd,kd->qk", query_h, key_h, preferred_element_type=jnp.float32) * 0.125
        scores = jnp.where(allowed, scores, -1e30)
        row_top = jnp.max(scores, axis=-1, keepdims=True)
        weights = jnp.exp(scores - row_top)
        row_total = jnp.sum(weights, axis=-1, keepdims=True)
        weights_low = (weights / row_total).astype(jnp.bfloat16)
        mixed_h = jnp.einsum("qk,kd->qd", weights_low, value_h, preferred_element_type=jnp.float32)
        return (mixed_h.astype(jnp.bfloat16), row_top[:, 0] + jnp.log(row_total[:, 0]))

    mixed_heads, log_totals = lax.map(attend, (query_heads, key_heads, value_heads))
    mixed = from_heads(mixed_heads)
    middle = (
        rows
        + tensor_sum(jnp.dot(mixed, proj_full, preferred_element_type=jnp.float32))
        + shift_vals[1]
    )
    normed_two, inv_two = layer_stats(middle)
    second_in = (normed_two * gain_vals[1] + shift_vals[2]).astype(jnp.bfloat16)
    hidden = (
        jnp.dot(second_in, up_full, preferred_element_type=jnp.float32) + bias_vals[2 * tp_width :]
    )
    sigma = jax.nn.sigmoid(1.702 * hidden)
    activated = (hidden * sigma).astype(jnp.bfloat16)
    output = (
        middle
        + tensor_sum(jnp.dot(activated, down_full, preferred_element_type=jnp.float32))
        + shift_vals[3]
    )
    grad_out = cotangent[0].astype(jnp.float32)
    grad_down_bias = jnp.sum(grad_out, axis=0)
    grad_branch = grad_out.astype(jnp.bfloat16)
    grad_down = jnp.einsum("tf,td->fd", activated, grad_branch, preferred_element_type=jnp.float32)
    grad_act = jnp.einsum("td,fd->tf", grad_branch, down_full, preferred_element_type=jnp.float32)
    grad_hidden = (grad_act * (sigma + 1.702 * hidden * sigma * (1.0 - sigma))).astype(jnp.bfloat16)
    grad_up_bias = jnp.sum(grad_hidden.astype(jnp.float32), axis=0)
    grad_up = jnp.einsum("td,tf->df", second_in, grad_hidden, preferred_element_type=jnp.float32)
    grad_second = tensor_sum(
        jnp.einsum("tf,df->td", grad_hidden, up_full, preferred_element_type=jnp.float32)
    )
    grad_gain_two = jnp.sum(grad_second * normed_two, axis=0)
    grad_shift_two = jnp.sum(grad_second, axis=0)
    grad_middle = grad_out + norm_back(grad_second, normed_two, inv_two, gain_vals[1])
    grad_proj_bias = jnp.sum(grad_middle, axis=0)
    grad_attn = grad_middle.astype(jnp.bfloat16)
    grad_proj = jnp.einsum("tc,td->cd", mixed, grad_attn, preferred_element_type=jnp.float32)
    grad_mixed = jnp.einsum(
        "td,cd->tc", grad_attn, proj_full, preferred_element_type=jnp.float32
    ).astype(jnp.bfloat16)

    def attend_back(head_items):
        query_h, key_h, value_h, grad_h, log_total = head_items
        scores = jnp.einsum("qd,kd->qk", query_h, key_h, preferred_element_type=jnp.float32) * 0.125
        weights = jnp.where(allowed, jnp.exp(scores - log_total[:, None]), 0.0)
        grad_weights = jnp.einsum("qd,kd->qk", grad_h, value_h, preferred_element_type=jnp.float32)
        row_delta = jnp.sum(weights * grad_weights, axis=-1, keepdims=True)
        grad_scores = (weights * (grad_weights - row_delta)).astype(jnp.bfloat16)
        grad_query_h = (
            jnp.einsum("qk,kd->qd", grad_scores, key_h, preferred_element_type=jnp.float32) * 0.125
        )
        grad_key_h = (
            jnp.einsum("qk,qd->kd", grad_scores, query_h, preferred_element_type=jnp.float32)
            * 0.125
        )
        grad_value_h = jnp.einsum(
            "qk,qd->kd", weights.astype(jnp.bfloat16), grad_h, preferred_element_type=jnp.float32
        )
        return (grad_query_h, grad_key_h, grad_value_h)

    query_parts, key_parts, value_parts = lax.map(
        attend_back, (query_heads, key_heads, value_heads, to_heads(grad_mixed), log_totals)
    )
    key_sum, value_sum = (
        lax.psum_scatter(from_heads(key_parts), "ctx", scatter_dimension=0, tiled=True),
        lax.psum_scatter(from_heads(value_parts), "ctx", scatter_dimension=0, tiled=True),
    )
    grad_query = from_heads(query_parts).astype(jnp.bfloat16)
    grad_key = key_sum.astype(jnp.bfloat16)
    grad_value = value_sum.astype(jnp.bfloat16)
    grad_qkv = jnp.stack(
        [
            jnp.einsum("td,tc->dc", first_in, grad_query, preferred_element_type=jnp.float32),
            jnp.einsum("td,tc->dc", first_in, grad_key, preferred_element_type=jnp.float32),
            jnp.einsum("td,tc->dc", first_in, grad_value, preferred_element_type=jnp.float32),
        ]
    )
    grad_head = jnp.concatenate(
        [
            jnp.sum(grad_query.astype(jnp.float32), axis=0),
            jnp.sum(grad_value.astype(jnp.float32), axis=0),
            grad_up_bias,
        ]
    )[None, :]
    grad_first_part = jnp.einsum(
        "tc,dc->td", grad_query, qkv_full[0], preferred_element_type=jnp.float32
    )
    grad_first_part = grad_first_part + jnp.einsum(
        "tc,dc->td", grad_key, qkv_full[1], preferred_element_type=jnp.float32
    )
    grad_first_part = grad_first_part + jnp.einsum(
        "tc,dc->td", grad_value, qkv_full[2], preferred_element_type=jnp.float32
    )
    grad_first = tensor_sum(grad_first_part)
    grad_gain_one = jnp.sum(grad_first * normed_one, axis=0)
    grad_shift_one = jnp.sum(grad_first, axis=0)
    grad_rows = grad_middle + norm_back(grad_first, normed_one, inv_one, gain_vals[0])
    grad_gains = jnp.stack([grad_gain_one, grad_gain_two])
    grad_shifts = jnp.stack([grad_shift_one, grad_proj_bias, grad_shift_two, grad_down_bias])
    share_gains, share_shifts, share_head, share_qkv, share_proj, share_up, share_down = (
        lax.psum_scatter(grad_gains, "fsdp", scatter_dimension=1, tiled=True),
        lax.psum_scatter(grad_shifts, "fsdp", scatter_dimension=1, tiled=True),
        lax.psum_scatter(grad_head, "fsdp", scatter_dimension=1, tiled=True),
        lax.psum_scatter(grad_qkv, "fsdp", scatter_dimension=1, tiled=True),
        lax.psum_scatter(grad_proj, "fsdp", scatter_dimension=1, tiled=True),
        lax.psum_scatter(grad_up, "fsdp", scatter_dimension=0, tiled=True),
        lax.psum_scatter(grad_down, "fsdp", scatter_dimension=1, tiled=True),
    )
    owned = lax.psum(
        (share_gains, share_shifts, share_head, share_qkv, share_proj, share_up, share_down), "ctx"
    )
    return (output.astype(jnp.bfloat16)[None], grad_rows[None]) + tuple(owned)


def on_device(
    image_input,
    image_segments,
    image_cotangent,
    image_gains,
    image_shifts,
    image_head_bias,
    image_qkv_weight,
    image_proj_weight,
    image_up_weight,
    image_down_weight,
    text_input,
    text_segments,
    text_cotangent,
    text_gains,
    text_shifts,
    text_head_bias,
    text_qkv_weight,
    text_proj_weight,
    text_up_weight,
    text_down_weight,
):
    image_results = run_block(
        image_input,
        image_segments,
        image_cotangent,
        image_gains,
        image_shifts,
        image_head_bias,
        image_qkv_weight,
        image_proj_weight,
        image_up_weight,
        image_down_weight,
        False,
    )
    text_results = run_block(
        text_input,
        text_segments,
        text_cotangent,
        text_gains,
        text_shifts,
        text_head_bias,
        text_qkv_weight,
        text_proj_weight,
        text_up_weight,
        text_down_weight,
        True,
    )
    return image_results + text_results


def solution(mesh):
    return jax.shard_map(
        on_device,
        mesh=mesh,
        in_specs=(
            P("fsdp", "ctx", None),
            P("fsdp", None),
            P("fsdp", "ctx", None),
            P(None, "fsdp"),
            P(None, "fsdp"),
            P("tp", "fsdp"),
            P(None, "fsdp", "tp"),
            P("tp", "fsdp"),
            P("fsdp", "tp"),
            P("tp", "fsdp"),
            P("fsdp", "ctx", None),
            P("fsdp", None),
            P("fsdp", "ctx", None),
            P(None, "fsdp"),
            P(None, "fsdp"),
            P("tp", "fsdp"),
            P(None, "fsdp", "tp"),
            P("tp", "fsdp"),
            P("fsdp", "tp"),
            P("tp", "fsdp"),
        ),
        out_specs=(
            P("fsdp", "ctx", None),
            P("fsdp", "ctx", None),
            P(None, "fsdp"),
            P(None, "fsdp"),
            P("tp", "fsdp"),
            P(None, "fsdp", "tp"),
            P("tp", "fsdp"),
            P("fsdp", "tp"),
            P("tp", "fsdp"),
            P("fsdp", "ctx", None),
            P("fsdp", "ctx", None),
            P(None, "fsdp"),
            P(None, "fsdp"),
            P("tp", "fsdp"),
            P(None, "fsdp", "tp"),
            P("tp", "fsdp"),
            P("fsdp", "tp"),
            P("tp", "fsdp"),
        ),
        check_vma=False,
    )
```

profile of v0, /device:TPU:0, one launch (start us, length us, event | category | flops | bytes accessed | tf_op | source)
XLA Modules:
  0.0 1437.0 jit_solution(6078367909397916896)
XLA Ops:
  8.0 9.5 all_gather.63
  33.9 16.2 %all_gather.65 = bf16[3,512,256]{2,1,0:T(8,128)(2,1)S(1)} all-gather(bf16[3,128,256]{2,1,0:T(8,128)(2,1)} %param.44), channel_id=1, replica_groups=mesh['fsdp'=4,'ctx'=4,'tp'=2] {'fsdp'}, dimensions={1}, use_global_device_ids=true | all-gather | bytes 983040 | tf_op jit(solution)/shard_map/all_gather | solution.py:46
  70.5 9.3 all-reduce
  93.6 9.8 all_gather.60
  116.6 30.7 %while.58 = (s32[]{:T(128)}, bf16[4,512,64]{1,2,0:T(8,128)(2,1)S(1)}, f32[4,512]{1,0:T(4,128)S(1)}, bf16[4,512,64]{2,1,0:T(8,128)(2,1)}, bf16[4,2048,64]{2,1,0:T...) while((s32[]{:T(128)}, ...), condition=%wide.region_49.50_spmd.clone, body=%wide.region_46.49_spmd.clone.sunk | while | flops 280002048 | bytes 30640268 | solution.py:105
  157.6 29.2 %all-gather.14.cloned.1.call-done = bf16[2048,384]{1,0:T(8,128)(2,1)} async-done(((bf16[512,384]{1,0:T(8,128)(2,1)}), bf16[2048,384]{1,0:T(8,128)(2,1)}) %all-gather.14.cloned.1.call-update) | async-done | bytes 1572880 | tf_op jit(solution)/shard_map/all_gather | solution.py:87
  193.5 43.0 %while.56 = (s32[]{:T(128)}, bf16[6,512,64]{1,2,0:T(8,128)(2,1)S(1)}, f32[6,512]{1,0:T(8,128)S(1)}, bf16[6,512,64]{2,1,0:T(8,128)(2,1)S(1)}, bf16[6,2048,64]{2,1...) while((s32[]{:T(128)}, ...), condition=%wide.region_5.6_spmd.clone, body=%wide.region_2.5_spmd.clone.sunk | while | flops 277904896 | bytes 30638212 | solution.py:105
  241.5 18.1 %all-reduce.17.cloned.1.call-done = (f32[512,768]{1,0:T(8,128)}, f32[512,512]{1,0:T(8,128)}) async-done(((f32[512,768]{1,0:T(8,128)}, f32[512,512]{1,0:T(8,128)}), (f32[512,768]{1,0:T(8,128)}, f32[512,512]{1,0:T(8,128)})) %all-reduce.17.cloned.1.call-update) | async-done | bytes 2621456 | tf_op jit(solution)/shard_map/psum | solution.py:26
  262.1 27.4 %all-gather.26.cloned.1.call-done = bf16[512,1024]{1,0:T(8,128)(2,1)} async-done(((bf16[128,1024]{1,0:T(8,128)(2,1)}), bf16[512,1024]{1,0:T(8,128)(2,1)}) %all-gather.26.cloned.1.call-update) | async-done | bytes 1048592 | tf_op jit(solution)/shard_map/all_gather | solution.py:48
  293.4 24.6 %all-gather.28.cloned.1.call-done = bf16[1024,512]{1,0:T(8,128)(2,1)} async-done(((bf16[1024,128]{1,0:T(8,128)(2,1)}), bf16[1024,512]{1,0:T(8,128)(2,1)}) %all-gather.28.cloned.1.call-update) | async-done | bytes 1048592 | tf_op jit(solution)/shard_map/all_gather | solution.py:49
  324.5 33.0 %all-gather.18.cloned.1.call-done = bf16[768,1536]{1,0:T(8,128)(2,1)} async-done(((bf16[192,1536]{1,0:T(8,128)(2,1)}), bf16[768,1536]{1,0:T(8,128)(2,1)}) %all-gather.18.cloned.1.call-update) | async-done | bytes 2359312 | tf_op jit(solution)/shard_map/all_gather | solution.py:48
  362.3 34.5 %all-gather.20.cloned.1.call-done = bf16[1536,768]{0,1:T(8,128)(2,1)} async-done(((bf16[1536,192]{0,1:T(8,128)(2,1)}), bf16[1536,768]{0,1:T(8,128)(2,1)}) %all-gather.20.cloned.1.call-update) | async-done | bytes 2359312 | tf_op jit(solution)/shard_map/all_gather | solution.py:49
  406.5 22.1 %all-reduce.15.cloned.1.call-done = (f32[512,768]{1,0:T(8,128)}, f32[512,512]{1,0:T(8,128)}) async-done(((f32[512,768]{1,0:T(8,128)}, f32[512,512]{1,0:T(8,128)}), (f32[512,768]{1,0:T(8,128)}, f32[512,512]{1,0:T(8,128)})) %all-reduce.15.cloned.1.call-update) | async-done | bytes 2621456 | tf_op jit(solution)/shard_map/psum | solution.py:26
  435.3 31.2 %while.59 = (s32[]{:T(128)}, bf16[4,512,64]{1,2,0:T(8,128)(2,1)S(1)}, f32[4,2048,64]{1,2,0:T(8,128)}, f32[4,2048,64]{1,2,0:T(8,128)}, bf16[4,512,64]{2,1,0:T(8,1...) while((s32[]{:T(128)}, ...), condition=%wide.region_59.60_spmd.clone, body=%wide.region_57.59_spmd.clone.sunk | while | flops 683834880 | bytes 40004792 | solution.py:164
  474.8 65.2 %while.57 = (s32[]{:T(128)}, bf16[6,512,64]{1,2,0:T(8,128)(2,1)}, f32[6,2048,64]{1,2,0:T(8,128)}, f32[6,2048,64]{1,2,0:T(8,128)}, bf16[6,512,64]{2,1,0:T(8,128)(...) while((s32[]{:T(128)}, bf16[6,512,64]{1,2,0:T(8,128)(2,1)}, ...), condition=%wide.region_15.16_spmd.clone, body=%wide.region_13.15_spmd.clone.sunk | while | flops 681737728 | bytes 34759800 | solution.py:164
  560.1 59.0 %reduce-scatter.31.cloned.1.call-done = f32[512,384]{0,1:T(8,128)} async-done(((f32[2048,384]{0,1:T(8,128)}), f32[512,384]{0,1:T(8,128)}) %reduce-scatter.31.cloned.1.call-update) | async-done | bytes 786448 | tf_op jit(solution)/shard_map/reduce_scatter | solution.py:168
  622.2 59.4 %reduce-scatter.33.cloned.1.call-done = f32[512,384]{0,1:T(8,128)} async-done(((f32[2048,384]{0,1:T(8,128)}), f32[512,384]{0,1:T(8,128)}) %reduce-scatter.33.cloned.1.call-update) | async-done | bytes 786448 | tf_op jit(solution)/shard_map/reduce_scatter | solution.py:169
  745.7 38.0 %reduce-scatter.51.cloned.1.call-done = f32[128,1024]{1,0:T(8,128)} async-done(((f32[512,1024]{1,0:T(8,128)}), f32[128,1024]{1,0:T(8,128)}) %reduce-scatter.51.cloned.1.call-update) | async-done | bytes 524304 | tf_op jit(solution)/shard_map/reduce_scatter | solution.py:209
  783.7 38.4 %reduce-scatter.53.cloned.1.call-done = f32[1024,128]{1,0:T(8,128)} async-done(((f32[1024,512]{1,0:T(8,128)}), f32[1024,128]{1,0:T(8,128)}) %reduce-scatter.53.cloned.1.call-update) | async-done | bytes 524304 | tf_op jit(solution)/shard_map/reduce_scatter | solution.py:210
  822.1 31.9 %reduce-scatter.37.cloned.1.call-done = f32[384,192]{0,1:T(8,128)} async-done(((f32[384,768]{0,1:T(8,128)}), f32[384,192]{0,1:T(8,128)}) %reduce-scatter.37.cloned.1.call-update) | async-done | bytes 294928 | tf_op jit(solution)/shard_map/reduce_scatter | solution.py:208
  854.1 60.1 %reduce-scatter.39.cloned.1.call-done = f32[192,1536]{1,0:T(8,128)} async-done(((f32[768,1536]{1,0:T(8,128)}), f32[192,1536]{1,0:T(8,128)}) %reduce-scatter.39.cloned.1.call-update) | async-done | bytes 1179664 | tf_op jit(solution)/shard_map/reduce_scatter | solution.py:209
  914.2 60.1 %reduce-scatter.41.cloned.1.call-done = f32[1536,192]{0,1:T(8,128)} async-done(((f32[1536,768]{0,1:T(8,128)}), f32[1536,192]{0,1:T(8,128)}) %reduce-scatter.41.cloned.1.call-update) | async-done | bytes 1179664 | tf_op jit(solution)/shard_map/reduce_scatter | solution.py:210
  974.3 34.0 %reduce-scatter.47.cloned.1.call-done = f32[3,128,256]{2,1,0:T(8,128)} async-done(((f32[3,512,256]{2,1,0:T(8,128)}), f32[3,128,256]{2,1,0:T(8,128)}) %reduce-scatter.47.cloned.1.call-update) | async-done | bytes 393232 | tf_op jit(solution)/shard_map/reduce_scatter | solution.py:207
  1008.3 50.2 %reduce-scatter.35.cloned.1.call-done = f32[3,192,384]{2,1,0:T(8,128)} async-done(((f32[3,768,384]{2,1,0:T(8,128)}), f32[3,192,384]{2,1,0:T(8,128)}) %reduce-scatter.35.cloned.1.call-update) | async-done | bytes 884752 | tf_op jit(solution)/shard_map/reduce_scatter | solution.py:207
  1058.5 29.6 %reduce-scatter.65.cloned.1.call-done = f32[384,1]{1,0:T(8,128)} async-done(((f32[1536,1]{1,0:T(8,128)}), f32[384,1]{1,0:T(8,128)}) %reduce-scatter.65.cloned.1.call-update) | async-done | bytes 1552
  1089.1 30.9 %reduce-scatter.59.cloned.1.call-done = f32[576,1]{1,0:T(8,128)} async-done(((f32[2304,1]{1,0:T(8,128)}), f32[576,1]{1,0:T(8,128)}) %reduce-scatter.59.cloned.1.call-update) | async-done | bytes 2320
  1128.9 18.4 %reduce-scatter.61.cloned.1.call-done = f32[128,2]{1,0:T(8,128)} async-done(((f32[512,2]{1,0:T(8,128)}), f32[128,2]{1,0:T(8,128)}) %reduce-scatter.61.cloned.1.call-update) | async-done | bytes 1040
  1148.2 27.1 %reduce-scatter.55.cloned.1.call-done = f32[192,2]{1,0:T(8,128)} async-done(((f32[768,2]{1,0:T(8,128)}), f32[192,2]{1,0:T(8,128)}) %reduce-scatter.55.cloned.1.call-update) | async-done | bytes 1552
  1176.3 26.7 %reduce-scatter.63.cloned.1.call-done = f32[128,4]{1,0:T(8,128)} async-done(((f32[512,4]{1,0:T(8,128)}), f32[128,4]{1,0:T(8,128)}) %reduce-scatter.63.cloned.1.call-update) | async-done | bytes 2064
  1203.9 26.8 %reduce-scatter.57.cloned.1.call-done = f32[192,4]{1,0:T(8,128)} async-done(((f32[768,4]{1,0:T(8,128)}), f32[192,4]{1,0:T(8,128)}) %reduce-scatter.57.cloned.1.call-update) | async-done | bytes 3088
  1231.6 21.5 %all-reduce.1 = (f32[2,192]{1,0:T(2,128)}, f32[4,192]{1,0:T(4,128)}, f32[1,576]{1,0:T(1,128)}, f32[2,128]{1,0:T(2,128)}, f32[4,128]{1,0:T(4,128)}, /*index=5*/f32[1,384]{1,0:T(1,128)}) all-reduce(f32[2,192]{1,0:T(2,128)S(1)} %copy.101, f32[4,192]{1,0:T(4,128)S(1)} %copy.103, ...), channel_id=1, replica_groups=mesh['fsdp'=4,'ctx'=4,'tp'=2] {'ctx'}, use_global_device_ids=true, to_apply=%region_24.25 | all-reduce | flops 2880 | bytes 23040 | tf_op jit(solution)/shard_map/psum | solution.py:212
  1253.1 167.8 %all-reduce.11.cloned.1.call-done = (f32[3,192,384]{2,1,0:T(8,128)}, f32[384,192]{0,1:T(8,128)}, f32[192,1536]{1,0:T(8,128)}, f32[1536,192]{0,1:T(8,128)}, f32[3...) async-done(((f32[3,192,384]{2,1,0:T(8,128)}, f32[384,192]{0,1:T(8,128)}, f32[192,1536]{1,0:T(8,128)}, f32[1536,192]{0,1:T(8,128)}, ...) | async-done | bytes 5111824 | tf_op jit(solution)/shard_map/psum | solution.py:212
  (558 shorter events, 406.1 us)
Async XLA Ops:
  7.2 73.8 %all-gather.12.cloned.1.call-start = ((), (), s32[]{:S(2)}) async-start(), calls=%async_computation.18 | async-start | bytes 2211840 | tf_op jit(solution)/shard_map/all_gather | solution.py:46
  7.9 95.5 %all-gather.24.cloned.1.call-start = ((), (), s32[]{:S(2)}) async-start(), calls=%async_computation.30 | async-start | bytes 1310720 | tf_op jit(solution)/shard_map/all_gather | solution.py:88
  52.4 57.8 %all-gather.22.cloned.1.call-start = ((), (), s32[]{:S(2)}) async-start(), calls=%async_computation.29 | async-start | bytes 1310720 | tf_op jit(solution)/shard_map/all_gather | solution.py:87
  53.5 97.3 %all-gather.16.cloned.1.call-start = ((), (), s32[]{:S(2)}) async-start(), calls=%async_computation.20 | async-start | bytes 1966080 | tf_op jit(solution)/shard_map/all_gather | solution.py:88
  80.4 277.1 %copy-start.80 = (f32[768]{0:T(1024)}, f32[768]{0:T(1024)S(1)}, u32[]{:S(2)}) copy-start(f32[768]{0:T(1024)S(1)} %get-tuple-element.447) | copy-start | bytes 9220
  83.6 103.2 %all-gather.14.cloned.1.call-start = ((), (), s32[]{:S(2)}) async-start(), calls=%async_computation.19 | async-start | bytes 1966080 | tf_op jit(solution)/shard_map/all_gather | solution.py:87
  116.0 143.6 %all-reduce.17.cloned.1.call-start = ((), (), s32[]{:S(2)}) async-start(), calls=%async_computation.48 | async-start | bytes 5242880 | tf_op jit(solution)/shard_map/psum | solution.py:26
  238.4 51.1 %all-gather.26.cloned.1.call-start = ((), (), s32[]{:S(2)}) async-start(), calls=%async_computation.31 | async-start | bytes 1310720 | tf_op jit(solution)/shard_map/all_gather | solution.py:48
  239.2 78.8 %all-gather.28.cloned.1.call-start = ((), (), s32[]{:S(2)}) async-start(), calls=%async_computation.32 | async-start | bytes 1310720 | tf_op jit(solution)/shard_map/all_gather | solution.py:49
  239.9 117.6 %all-gather.18.cloned.1.call-start = ((), (), s32[]{:S(2)}) async-start(), calls=%async_computation.21 | async-start | bytes 2949120 | tf_op jit(solution)/shard_map/all_gather | solution.py:48
  240.7 156.2 %all-gather.20.cloned.1.call-start = ((), (), s32[]{:S(2)}) async-start(), calls=%async_computation.22 | async-start | bytes 2949120 | tf_op jit(solution)/shard_map/all_gather | solution.py:49
  241.3 187.3 %all-reduce.15.cloned.1.call-start = ((), (), s32[]{:S(2)}) async-start(), calls=%async_computation.47 | async-start | bytes 5242880 | tf_op jit(solution)/shard_map/psum | solution.py:26
  406.2 147.4 %reduce-scatter.43.cloned.1.call-start = ((), (), s32[]{:S(2)}) async-start(), calls=%async_computation.33 | async-start | bytes 2621440 | tf_op jit(solution)/shard_map/reduce_scatter | solution.py:168
  466.5 90.8 %reduce-scatter.45.cloned.1.call-start = ((), (), s32[]{:S(2)}) async-start(), calls=%async_computation.34 | async-start | bytes 2621440 | tf_op jit(solution)/shard_map/reduce_scatter | solution.py:169
  474.8 144.3 %reduce-scatter.31.cloned.1.call-start = ((), (), s32[]{:S(2)}) async-start(), calls=%async_computation.23 | async-start | bytes 3932160 | tf_op jit(solution)/shard_map/reduce_scatter | solution.py:168
  540.0 141.6 %reduce-scatter.33.cloned.1.call-start = ((), (), s32[]{:S(2)}) async-start(), calls=%async_computation.24 | async-start | bytes 3932160 | tf_op jit(solution)/shard_map/reduce_scatter | solution.py:169
  540.6 192.2 %all-reduce.13.cloned.1.call-start = ((), (), s32[]{:S(2)}) async-start(), calls=%async_computation.46 | async-start | bytes 10485760 | tf_op jit(solution)/shard_map/psum | solution.py:26
  685.7 60.0 %reduce-scatter.49.cloned.1.call-start = ((), (), s32[]{:S(2)}) async-start(), calls=%async_computation.36 | async-start | bytes 655360 | tf_op jit(solution)/shard_map/reduce_scatter | solution.py:208
  688.9 94.8 %reduce-scatter.51.cloned.1.call-start = ((), (), s32[]{:S(2)}) async-start(), calls=%async_computation.37 | async-start | bytes 2621440 | tf_op jit(solution)/shard_map/reduce_scatter | solution.py:209
  692.5 129.7 %reduce-scatter.53.cloned.1.call-start = ((), (), s32[]{:S(2)}) async-start(), calls=%async_computation.38 | async-start | bytes 2621440 | tf_op jit(solution)/shard_map/reduce_scatter | solution.py:210
  697.1 157.0 %reduce-scatter.37.cloned.1.call-start = ((), (), s32[]{:S(2)}) async-start(), calls=%async_computation.26 | async-start | bytes 1474560 | tf_op jit(solution)/shard_map/reduce_scatter | solution.py:208
  700.3 213.9 %reduce-scatter.39.cloned.1.call-start = ((), (), s32[]{:S(2)}) async-start(), calls=%async_computation.27 | async-start | bytes 5898240 | tf_op jit(solution)/shard_map/reduce_scatter | solution.py:209
  705.5 268.8 %reduce-scatter.41.cloned.1.call-start = ((), (), s32[]{:S(2)}) async-start(), calls=%async_computation.28 | async-start | bytes 5898240 | tf_op jit(solution)/shard_map/reduce_scatter | solution.py:210
  712.9 295.3 %reduce-scatter.47.cloned.1.call-start = ((), (), s32[]{:S(2)}) async-start(), calls=%async_computation.35 | async-start | bytes 1966080 | tf_op jit(solution)/shard_map/reduce_scatter | solution.py:207
  718.9 339.6 %reduce-scatter.35.cloned.1.call-start = ((), (), s32[]{:S(2)}) async-start(), calls=%async_computation.25 | async-start | bytes 4423680 | tf_op jit(solution)/shard_map/reduce_scatter | solution.py:207
  725.1 362.9 %reduce-scatter.65.cloned.1.call-start = ((), (), s32[]{:S(2)}) async-start(), calls=%async_computation.44 | async-start | bytes 983040
  730.0 390.0 %reduce-scatter.59.cloned.1.call-start = ((), (), s32[]{:S(2)}) async-start(), calls=%async_computation.41 | async-start | bytes 1474560
  732.7 414.5 %reduce-scatter.61.cloned.1.call-start = ((), (), s32[]{:S(2)}) async-start(), calls=%async_computation.42 | async-start | bytes 327680
  736.7 438.6 %reduce-scatter.55.cloned.1.call-start = ((), (), s32[]{:S(2)}) async-start(), calls=%async_computation.39 | async-start | bytes 491520
  737.7 465.3 %reduce-scatter.63.cloned.1.call-start = ((), (), s32[]{:S(2)}) async-start(), calls=%async_computation.43 | async-start | bytes 327680
  738.7 492.0 %reduce-scatter.57.cloned.1.call-start = ((), (), s32[]{:S(2)}) async-start(), calls=%async_computation.40 | async-start | bytes 491520
  739.7 681.2 %all-reduce.11.cloned.1.call-start = ((), (), s32[]{:S(2)}) async-start(), calls=%async_computation.45 | async-start | bytes 10223616 | tf_op jit(solution)/shard_map/psum | solution.py:212
  (105 other events, 1003.5 us)
Sparse Core Ops, SparseCore 0:
  9.9 39.6 all-gather.11
  52.6 27.9 all-gather.23
  82.7 27.4 all-gather.21
  112.2 36.5 all-gather.15
  150.8 35.9 all-gather.13
  238.5 21.0 all-reduce.16
  261.6 27.8 all-gather.25
  291.5 26.4 all-gather.27
  320.0 37.4 all-gather.17
  359.3 37.4 all-gather.19
  406.4 22.1 all-reduce.14
  466.7 45.0 reduce-scatter.42
  514.2 43.1 reduce-scatter.44
  559.5 59.5 reduce-scatter.30
  621.3 60.2 reduce-scatter.32
  685.8 30.3 all-reduce.12
  719.6 25.9 reduce-scatter.48
  748.5 35.1 reduce-scatter.50
  786.9 35.1 reduce-scatter.52
  825.5 28.5 reduce-scatter.36
  857.1 57.0 reduce-scatter.38
  917.2 57.0 reduce-scatter.40
  977.3 30.9 reduce-scatter.46
  1011.2 47.2 reduce-scatter.34
  1062.0 26.0 reduce-scatter.64
  1091.4 28.4 reduce-scatter.58
  1123.1 24.0 reduce-scatter.60
  1150.9 24.4 reduce-scatter.54
  1178.9 24.0 reduce-scatter.62
  1206.2 24.4 reduce-scatter.56
  1233.6 187.2 all-reduce.10
where the time goes:
time: 1450 us; the launch traced here: 1440 us
  waiting for transfers between devices  962 us (66%)
  matrix products  238 us (16%)
  blocking collectives  105 us (7%)
  local copies, waits for them, and re-layouts  70.3 us (5%)
  other arithmetic  41.6 us (3%)
  between operations  16.6 us (1%)
    psum x1, waiting for transfers between devices, run_block(): lax.psum((share_gains, share_shifts, share_head, share_qkv, share_proj, s...  168 us
    unnamed x37, waiting for transfers between devices  164 us
    reduce_scatter x2, waiting for transfers between devices, run_block(): lax.psum_scatter(grad_down, 'fsdp', scatter_dimension=1, tiled=True)  98.6 us
    reduce_scatter x2, waiting for transfers between devices, run_block(): lax.psum_scatter(grad_up, 'fsdp', scatter_dimension=0, tiled=True)  98.2 us
    reduce_scatter x2, waiting for transfers between devices, run_block(): lax.psum_scatter(grad_qkv, 'fsdp', scatter_dimension=1, tiled=True)  84.1 us
    reduce_scatter x2, waiting for transfers between devices, run_block(): lax.psum_scatter(from_heads(value_parts), 'ctx', scatter_dimension=0, til...  60.4 us
    all_gather x2, waiting for transfers between devices, run_block(): lax.all_gather(up_weight, 'fsdp', axis=0, tiled=True)  60.4 us
    all_gather x2, waiting for transfers between devices, run_block(): lax.all_gather(down_weight, 'fsdp', axis=1, tiled=True)  59.1 us
  transfers between devices with their start and end apart: 31, of which 26 were waited for; matrix products, arithmetic and copies ran while one was open for 16% of the time, Pallas kernels for 0%

commit v1 on v0

--- a/solution.py
+++ b/solution.py
@@ -4,6 +4,28 @@
 from jax.sharding import PartitionSpec as P
 
 HD = 64
+
+
+def laid_out(blocks, dim):
+    lengths = list(blocks.shape[1:])
+    lengths[dim] *= blocks.shape[0]
+    return jnp.moveaxis(blocks, 0, dim).reshape(lengths)
+
+
+def collect(x, axis, dim):
+    size = lax.axis_size(axis)
+    pairs = [(i, (i + 1) % size) for i in range(size)]
+    back = [(b, a) for a, b in pairs]
+    lower, upper = ([], [])
+    for step in range(size - 1):
+        if step % 2 == 0:
+            lower.append(lax.ppermute(lower[-1] if lower else x, axis, pairs))
+        else:
+            upper.append(lax.ppermute(upper[-1] if upper else x, axis, back))
+    parts = jnp.stack([*lower[::-1], x, *upper])
+    shift = lax.axis_index(axis) - len(lower)
+    parts = parts[(jnp.arange(size) - shift) % size]
+    return laid_out(parts, dim)
 
 
 def layer_stats(rows):
@@ -46,7 +68,7 @@
         lax.all_gather(qkv_weight, "fsdp", axis=1, tiled=True),
         lax.all_gather(proj_weight, "fsdp", axis=1, tiled=True),
         lax.all_gather(up_weight, "fsdp", axis=0, tiled=True),
-        lax.all_gather(down_weight, "fsdp", axis=1, tiled=True),
+        collect(down_weight, "fsdp", 1),
     )
     gain_vals = gain_full.astype(jnp.float32)
     shift_vals = shift_full.astype(jnp.float32)

time: 1450 us -> 1390 us (0.959)
  waiting for transfers between devices: 962 us -> 894 us
    all_gather x2 -> x0, waiting for transfers between devices: 59.1 us -> none  [run_block(): lax.all_gather(down_weight, 'fsdp', axis=1, tiled=True)]
    ppermute x0 -> x6, waiting for transfers between devices: none -> 58.4 us  [the longest x2 38.5 us: collect(): upper.append(lax.ppermute(upper[-1] if upper else x, axis, back))]
    all_gather x2, waiting for transfers between devices: 60.4 us -> 13.5 us  [run_block(): lax.all_gather(up_weight, 'fsdp', axis=0, tiled=True)]
    psum x3, waiting for transfers between devices: 40.2 us -> 22.1 us  [tensor_sum(): return lax.psum(partial_rows, 'tp')]
    unnamed x37 -> x35, waiting for transfers between devices: 164 us -> 162 us
    unnamed x203 -> x215, local copies, waits for them, and re-layouts: 43.6 us -> 42.3 us
  transfers between devices with their start and end apart: 31 -> 35, of which waited for: 26 -> 26; matrix products, arithmetic and copies ran while one was open for 16% -> 16% of each run, Pallas kernels for 0% -> 0%
where the time goes in v1:
time: 1390 us; the launch traced here: 1380 us
  waiting for transfers between devices  894 us (64%)
  matrix products  232 us (17%)
  blocking collectives  105 us (8%)
  local copies, waits for them, and re-layouts  75.9 us (5%)
  other arithmetic  45.1 us (3%)
  between operations  16.4 us (1%)
    psum x1, waiting for transfers between devices, run_block(): lax.psum((share_gains, share_shifts, share_head, share_qkv, share_proj, s...  168 us
    unnamed x35, waiting for transfers between devices  162 us
    reduce_scatter x2, waiting for transfers between devices, run_block(): lax.psum_scatter(grad_down, 'fsdp', scatter_dimension=1, tiled=True)  98.3 us
    reduce_scatter x2, waiting for transfers between devices, run_block(): lax.psum_scatter(grad_up, 'fsdp', scatter_dimension=0, tiled=True)  98.2 us
    reduce_scatter x2, waiting for transfers between devices, run_block(): lax.psum_scatter(grad_qkv, 'fsdp', scatter_dimension=1, tiled=True)  84.3 us
    reduce_scatter x2, waiting for transfers between devices, run_block(): lax.psum_scatter(from_heads(value_parts), 'ctx', scatter_dimension=0, til...  60.4 us
    reduce_scatter x2, waiting for transfers between devices, run_block(): lax.psum_scatter(from_heads(key_parts), 'ctx', scatter_dimension=0, tiled...  59 us
    unnamed x215, local copies, waits for them, and re-layouts  42.3 us
  transfers between devices with their start and end apart: 35, of which 26 were waited for; matrix products, arithmetic and copies ran while one was open for 16% of the time, Pallas kernels for 0%

profile of v1, /device:TPU:0, one launch (start us, length us, event | category | flops | bytes accessed | tf_op | source)
XLA Modules:
  0.0 1379.9 jit_solution(3189334577939901383)
XLA Ops:
  8.0 9.5 all_gather.56
  17.5 7.9 all_gather.59
  33.9 16.2 %all_gather.58 = bf16[3,512,256]{2,1,0:T(8,128)(2,1)S(1)} all-gather(bf16[3,128,256]{2,1,0:T(8,128)(2,1)} %param.44), channel_id=1, replica_groups=mesh['fsdp'=4,'ctx'=4,'tp'=2] {'fsdp'}, dimensions={1}, use_global_device_ids=true | all-gather | bytes 983040 | tf_op jit(solution)/shard_map/all_gather | solution.py:68
  70.5 9.3 all-reduce
  85.0 8.5 all_gather.62
  93.6 9.8 all_gather.54
  116.6 31.1 %while.58 = (s32[]{:T(128)}, bf16[4,512,64]{1,2,0:T(8,128)(2,1)S(1)}, f32[4,512]{1,0:T(4,128)S(1)}, bf16[4,512,64]{2,1,0:T(8,128)(2,1)}, bf16[4,2048,64]{2,1,0:T...) while((s32[]{:T(128)}, ...), condition=%wide.region_49.50_spmd.clone, body=%wide.region_46.49_spmd.clone.sunk | while | flops 280002048 | bytes 30640268 | solution.py:127
  158.1 28.8 %all-gather.12.cloned.1.call-done = bf16[2048,384]{1,0:T(8,128)(2,1)} async-done(((bf16[512,384]{1,0:T(8,128)(2,1)}), bf16[2048,384]{1,0:T(8,128)(2,1)}) %all-gather.12.cloned.1.call-update) | async-done | bytes 1572880 | tf_op jit(solution)/shard_map/all_gather | solution.py:109
  193.6 43.7 %while.56 = (s32[]{:T(128)}, bf16[6,512,64]{1,2,0:T(8,128)(2,1)S(1)}, f32[6,512]{1,0:T(8,128)S(1)}, bf16[6,512,64]{2,1,0:T(8,128)(2,1)S(1)}, bf16[6,2048,64]{2,1...) while((s32[]{:T(128)}, ...), condition=%wide.region_5.6_spmd.clone, body=%wide.region_2.5_spmd.clone.sunk | while | flops 277904896 | bytes 30638212 | solution.py:127
  244.4 13.0 collective-permute-done
  263.8 38.5 %collective-permute-done.5 = bf16[1024,128]{1,0:T(8,128)(2,1)S(1)} collective-permute-done((bf16[1024,128]{1,0:T(8,128)(2,1)S(1)}, bf16[1024,128]{1,0:T(8,128)(2,1)S(1)}, u32[]{:S(2)}, u32[]{:S(2)}) %collective-permute-start.5) | collective-permute-done | bytes 262176 | tf_op jit(solution)/shard_map/ppermute | solution.py:24
  324.8 13.4 all-gather.16.cloned.1.call-done
  349.8 22.1 %all-reduce.15.cloned.1.call-done = (f32[512,768]{1,0:T(8,128)}, f32[512,512]{1,0:T(8,128)}) async-done(((f32[512,768]{1,0:T(8,128)}, f32[512,512]{1,0:T(8,128)}), (f32[512,768]{1,0:T(8,128)}, f32[512,512]{1,0:T(8,128)})) %all-reduce.15.cloned.1.call-update) | async-done | bytes 2621456 | tf_op jit(solution)/shard_map/psum | solution.py:48
  378.6 31.1 %while.59 = (s32[]{:T(128)}, bf16[4,512,64]{1,2,0:T(8,128)(2,1)S(1)}, f32[4,2048,64]{1,2,0:T(8,128)}, f32[4,2048,64]{1,2,0:T(8,128)}, bf16[4,512,64]{2,1,0:T(8,1...) while((s32[]{:T(128)}, ...), condition=%wide.region_59.60_spmd.clone, body=%wide.region_57.59_spmd.clone.sunk | while | flops 683834880 | bytes 40004792 | solution.py:186
  418.0 65.1 %while.57 = (s32[]{:T(128)}, bf16[6,512,64]{1,2,0:T(8,128)(2,1)}, f32[6,2048,64]{1,2,0:T(8,128)}, f32[6,2048,64]{1,2,0:T(8,128)}, bf16[6,512,64]{2,1,0:T(8,128)(...) while((s32[]{:T(128)}, bf16[6,512,64]{1,2,0:T(8,128)(2,1)}, ...), condition=%wide.region_15.16_spmd.clone, body=%wide.region_13.15_spmd.clone.sunk | while | flops 681737728 | bytes 34759800 | solution.py:186
  503.3 59.0 %reduce-scatter.31.cloned.1.call-done = f32[512,384]{0,1:T(8,128)} async-done(((f32[2048,384]{0,1:T(8,128)}), f32[512,384]{0,1:T(8,128)}) %reduce-scatter.31.cloned.1.call-update) | async-done | bytes 786448 | tf_op jit(solution)/shard_map/reduce_scatter | solution.py:190
  565.4 59.5 %reduce-scatter.33.cloned.1.call-done = f32[512,384]{0,1:T(8,128)} async-done(((f32[2048,384]{0,1:T(8,128)}), f32[512,384]{0,1:T(8,128)}) %reduce-scatter.33.cloned.1.call-update) | async-done | bytes 786448 | tf_op jit(solution)/shard_map/reduce_scatter | solution.py:191
  689.1 38.1 %reduce-scatter.51.cloned.1.call-done = f32[128,1024]{1,0:T(8,128)} async-done(((f32[512,1024]{1,0:T(8,128)}), f32[128,1024]{1,0:T(8,128)}) %reduce-scatter.51.cloned.1.call-update) | async-done | bytes 524304 | tf_op jit(solution)/shard_map/reduce_scatter | solution.py:231
  727.1 38.3 %reduce-scatter.53.cloned.1.call-done = f32[1024,128]{1,0:T(8,128)} async-done(((f32[1024,512]{1,0:T(8,128)}), f32[1024,128]{1,0:T(8,128)}) %reduce-scatter.53.cloned.1.call-update) | async-done | bytes 524304 | tf_op jit(solution)/shard_map/reduce_scatter | solution.py:232
  765.4 31.9 %reduce-scatter.37.cloned.1.call-done = f32[384,192]{0,1:T(8,128)} async-done(((f32[384,768]{0,1:T(8,128)}), f32[384,192]{0,1:T(8,128)}) %reduce-scatter.37.cloned.1.call-update) | async-done | bytes 294928 | tf_op jit(solution)/shard_map/reduce_scatter | solution.py:230
  797.3 60.1 %reduce-scatter.39.cloned.1.call-done = f32[192,1536]{1,0:T(8,128)} async-done(((f32[768,1536]{1,0:T(8,128)}), f32[192,1536]{1,0:T(8,128)}) %reduce-scatter.39.cloned.1.call-update) | async-done | bytes 1179664 | tf_op jit(solution)/shard_map/reduce_scatter | solution.py:231
  857.5 60.0 %reduce-scatter.41.cloned.1.call-done = f32[1536,192]{0,1:T(8,128)} async-done(((f32[1536,768]{0,1:T(8,128)}), f32[1536,192]{0,1:T(8,128)}) %reduce-scatter.41.cloned.1.call-update) | async-done | bytes 1179664 | tf_op jit(solution)/shard_map/reduce_scatter | solution.py:232
  917.4 33.9 %reduce-scatter.47.cloned.1.call-done = f32[3,128,256]{2,1,0:T(8,128)} async-done(((f32[3,512,256]{2,1,0:T(8,128)}), f32[3,128,256]{2,1,0:T(8,128)}) %reduce-scatter.47.cloned.1.call-update) | async-done | bytes 393232 | tf_op jit(solution)/shard_map/reduce_scatter | solution.py:229
  951.4 50.3 %reduce-scatter.35.cloned.1.call-done = f32[3,192,384]{2,1,0:T(8,128)} async-done(((f32[3,768,384]{2,1,0:T(8,128)}), f32[3,192,384]{2,1,0:T(8,128)}) %reduce-scatter.35.cloned.1.call-update) | async-done | bytes 884752 | tf_op jit(solution)/shard_map/reduce_scatter | solution.py:229
  1001.7 29.6 %reduce-scatter.65.cloned.1.call-done = f32[384,1]{1,0:T(8,128)} async-done(((f32[1536,1]{1,0:T(8,128)}), f32[384,1]{1,0:T(8,128)}) %reduce-scatter.65.cloned.1.call-update) | async-done | bytes 1552
  1032.3 30.9 %reduce-scatter.59.cloned.1.call-done = f32[576,1]{1,0:T(8,128)} async-done(((f32[2304,1]{1,0:T(8,128)}), f32[576,1]{1,0:T(8,128)}) %reduce-scatter.59.cloned.1.call-update) | async-done | bytes 2320
  1072.1 18.6 %reduce-scatter.61.cloned.1.call-done = f32[128,2]{1,0:T(8,128)} async-done(((f32[512,2]{1,0:T(8,128)}), f32[128,2]{1,0:T(8,128)}) %reduce-scatter.61.cloned.1.call-update) | async-done | bytes 1040
  1091.6 27.0 %reduce-scatter.55.cloned.1.call-done = f32[192,2]{1,0:T(8,128)} async-done(((f32[768,2]{1,0:T(8,128)}), f32[192,2]{1,0:T(8,128)}) %reduce-scatter.55.cloned.1.call-update) | async-done | bytes 1552
  1119.5 26.5 %reduce-scatter.63.cloned.1.call-done = f32[128,4]{1,0:T(8,128)} async-done(((f32[512,4]{1,0:T(8,128)}), f32[128,4]{1,0:T(8,128)}) %reduce-scatter.63.cloned.1.call-update) | async-done | bytes 2064
  1147.0 26.9 %reduce-scatter.57.cloned.1.call-done = f32[192,4]{1,0:T(8,128)} async-done(((f32[768,4]{1,0:T(8,128)}), f32[192,4]{1,0:T(8,128)}) %reduce-scatter.57.cloned.1.call-update) | async-done | bytes 3088
  1174.8 21.5 %all-reduce.1 = (f32[2,192]{1,0:T(2,128)}, f32[4,192]{1,0:T(4,128)}, f32[1,576]{1,0:T(1,128)}, f32[2,128]{1,0:T(2,128)}, f32[4,128]{1,0:T(4,128)}, /*index=5*/f32[1,384]{1,0:T(1,128)}) all-reduce(f32[2,192]{1,0:T(2,128)S(1)} %copy.122, f32[4,192]{1,0:T(4,128)S(1)} %copy.124, ...), channel_id=1, replica_groups=mesh['fsdp'=4,'ctx'=4,'tp'=2] {'ctx'}, use_global_device_ids=true, to_apply=%region_24.25 | all-reduce | flops 2880 | bytes 23040 | tf_op jit(solution)/shard_map/psum | solution.py:234
  1196.3 167.8 %all-reduce.11.cloned.1.call-done = (f32[3,192,384]{2,1,0:T(8,128)}, f32[384,192]{0,1:T(8,128)}, f32[192,1536]{1,0:T(8,128)}, f32[1536,192]{0,1:T(8,128)}, f32[3...) async-done(((f32[3,192,384]{2,1,0:T(8,128)}, f32[384,192]{0,1:T(8,128)}, f32[192,1536]{1,0:T(8,128)}, f32[1536,192]{0,1:T(8,128)}, ...) | async-done | bytes 5111824 | tf_op jit(solution)/shard_map/psum | solution.py:234
  (583 shorter events, 405.8 us)
Async XLA Ops:
  7.2 73.8 %all-gather.10.cloned.1.call-start = ((), (), s32[]{:S(2)}) async-start(), calls=%async_computation.18 | async-start | bytes 2211840 | tf_op jit(solution)/shard_map/all_gather | solution.py:68
  7.9 95.5 %all-gather.20.cloned.1.call-start = ((), (), s32[]{:S(2)}) async-start(), calls=%async_computation.29 | async-start | bytes 1310720 | tf_op jit(solution)/shard_map/all_gather | solution.py:110
  52.4 57.8 %all-gather.18.cloned.1.call-start = ((), (), s32[]{:S(2)}) async-start(), calls=%async_computation.28 | async-start | bytes 1310720 | tf_op jit(solution)/shard_map/all_gather | solution.py:109
  53.5 97.8 %all-gather.14.cloned.1.call-start = ((), (), s32[]{:S(2)}) async-start(), calls=%async_computation.20 | async-start | bytes 1966080 | tf_op jit(solution)/shard_map/all_gather | solution.py:110
  83.6 103.3 %all-gather.12.cloned.1.call-start = ((), (), s32[]{:S(2)}) async-start(), calls=%async_computation.19 | async-start | bytes 1966080 | tf_op jit(solution)/shard_map/all_gather | solution.py:109
  116.1 200.0 %all-reduce.17.cloned.1.call-start = ((), (), s32[]{:S(2)}) async-start(), calls=%async_computation.46 | async-start | bytes 5242880 | tf_op jit(solution)/shard_map/psum | solution.py:48
  239.2 79.4 %all-gather.22.cloned.1.call-start = ((), (), s32[]{:S(2)}) async-start(), calls=%async_computation.30 | async-start | bytes 1310720 | tf_op jit(solution)/shard_map/all_gather | solution.py:70
  239.9 98.3 %all-gather.16.cloned.1.call-start = ((), (), s32[]{:S(2)}) async-start(), calls=%async_computation.21 | async-start | bytes 2949120 | tf_op jit(solution)/shard_map/all_gather | solution.py:70
  242.9 65.9 %collective-permute-start.2 = (bf16[1536,192]{0,1:T(8,128)(2,1)}, bf16[1536,192]{0,1:T(8,128)(2,1)}, u32[]{:S(2)}, u32[]{:S(2)}) collective-permute-start(bf16[1536,192]{0,1:T(8,128)(2,1)} %param.37), channel_id=1, source_target_pairs={{8,0},{16,8},{24,16},{0,24},{9,1},{17,9},{25,17},{1,25},{10,2},{18... | collective-permute-start | bytes 1769480 | tf_op jit(solution)/shard_map/ppermute | solution.py:24
  257.5 51.4 %collective-permute-start.1 = (bf16[1536,192]{0,1:T(8,128)(2,1)}, bf16[1536,192]{0,1:T(8,128)(2,1)}, u32[]{:S(2)}, u32[]{:S(2)}) collective-permute-start(bf16[1536,192]{0,1:T(8,128)(2,1)} %collective-permute-done), channel_id=1, source_target_pairs={{0,8},{8,16},{16,24},{24,0},{1,9},{9,17},{17,25},{25,1},{2,10},{10... | collective-permute-start | bytes 1769480 | tf_op jit(solution)/shard_map/ppermute | solution.py:22
  258.0 44.3 %collective-permute-start.5 = (bf16[1024,128]{1,0:T(8,128)(2,1)S(1)}, bf16[1024,128]{1,0:T(8,128)(2,1)S(1)}, u32[]{:S(2)}, u32[]{:S(2)}) collective-permute-start(bf16[1024,128]{1,0:T(8,128)(2,1)S(1)} %copy-done.54), channel_id=1, source_target_pairs={{8,0},{16,8},{24,16},{0,24},{9,1},{17,9},{25,17},{1,25},{10,2},{18... | collective-permute-start | bytes 786440 | tf_op jit(solution)/shard_map/ppermute | solution.py:24
  260.4 111.5 %all-reduce.15.cloned.1.call-start = ((), (), s32[]{:S(2)}) async-start(), calls=%async_computation.45 | async-start | bytes 5242880 | tf_op jit(solution)/shard_map/psum | solution.py:48
  349.5 147.5 %reduce-scatter.43.cloned.1.call-start = ((), (), s32[]{:S(2)}) async-start(), calls=%async_computation.31 | async-start | bytes 2621440 | tf_op jit(solution)/shard_map/reduce_scatter | solution.py:190
  409.8 90.8 %reduce-scatter.45.cloned.1.call-start = ((), (), s32[]{:S(2)}) async-start(), calls=%async_computation.32 | async-start | bytes 2621440 | tf_op jit(solution)/shard_map/reduce_scatter | solution.py:191
  418.0 144.4 %reduce-scatter.31.cloned.1.call-start = ((), (), s32[]{:S(2)}) async-start(), calls=%async_computation.22 | async-start | bytes 3932160 | tf_op jit(solution)/shard_map/reduce_scatter | solution.py:190
  483.1 141.9 %reduce-scatter.33.cloned.1.call-start = ((), (), s32[]{:S(2)}) async-start(), calls=%async_computation.23 | async-start | bytes 3932160 | tf_op jit(solution)/shard_map/reduce_scatter | solution.py:191
  483.9 192.4 %all-reduce.13.cloned.1.call-start = ((), (), s32[]{:S(2)}) async-start(), calls=%async_computation.44 | async-start | bytes 10485760 | tf_op jit(solution)/shard_map/psum | solution.py:48
  629.1 60.0 %reduce-scatter.49.cloned.1.call-start = ((), (), s32[]{:S(2)}) async-start(), calls=%async_computation.34 | async-start | bytes 655360 | tf_op jit(solution)/shard_map/reduce_scatter | solution.py:230
  632.3 94.8 %reduce-scatter.51.cloned.1.call-start = ((), (), s32[]{:S(2)}) async-start(), calls=%async_computation.35 | async-start | bytes 2621440 | tf_op jit(solution)/shard_map/reduce_scatter | solution.py:231
  635.9 129.6 %reduce-scatter.53.cloned.1.call-start = ((), (), s32[]{:S(2)}) async-start(), calls=%async_computation.36 | async-start | bytes 2621440 | tf_op jit(solution)/shard_map/reduce_scatter | solution.py:232
  640.5 156.9 %reduce-scatter.37.cloned.1.call-start = ((), (), s32[]{:S(2)}) async-start(), calls=%async_computation.25 | async-start | bytes 1474560 | tf_op jit(solution)/shard_map/reduce_scatter | solution.py:230
  643.7 213.7 %reduce-scatter.39.cloned.1.call-start = ((), (), s32[]{:S(2)}) async-start(), calls=%async_computation.26 | async-start | bytes 5898240 | tf_op jit(solution)/shard_map/reduce_scatter | solution.py:231
  649.0 268.4 %reduce-scatter.41.cloned.1.call-start = ((), (), s32[]{:S(2)}) async-start(), calls=%async_computation.27 | async-start | bytes 5898240 | tf_op jit(solution)/shard_map/reduce_scatter | solution.py:232
  656.4 294.9 %reduce-scatter.47.cloned.1.call-start = ((), (), s32[]{:S(2)}) async-start(), calls=%async_computation.33 | async-start | bytes 1966080 | tf_op jit(solution)/shard_map/reduce_scatter | solution.py:229
  662.4 339.3 %reduce-scatter.35.cloned.1.call-start = ((), (), s32[]{:S(2)}) async-start(), calls=%async_computation.24 | async-start | bytes 4423680 | tf_op jit(solution)/shard_map/reduce_scatter | solution.py:229
  668.6 362.7 %reduce-scatter.65.cloned.1.call-start = ((), (), s32[]{:S(2)}) async-start(), calls=%async_computation.42 | async-start | bytes 983040
  673.4 389.8 %reduce-scatter.59.cloned.1.call-start = ((), (), s32[]{:S(2)}) async-start(), calls=%async_computation.39 | async-start | bytes 1474560
  676.2 414.4 %reduce-scatter.61.cloned.1.call-start = ((), (), s32[]{:S(2)}) async-start(), calls=%async_computation.40 | async-start | bytes 327680
  680.1 438.4 %reduce-scatter.55.cloned.1.call-start = ((), (), s32[]{:S(2)}) async-start(), calls=%async_computation.37 | async-start | bytes 491520
  681.2 464.9 %reduce-scatter.63.cloned.1.call-start = ((), (), s32[]{:S(2)}) async-start(), calls=%async_computation.41 | async-start | bytes 327680
  682.2 491.7 %reduce-scatter.57.cloned.1.call-start = ((), (), s32[]{:S(2)}) async-start(), calls=%async_computation.38 | async-start | bytes 491520
  683.2 680.9 %all-reduce.11.cloned.1.call-start = ((), (), s32[]{:S(2)}) async-start(), calls=%async_computation.43 | async-start | bytes 10223616 | tf_op jit(solution)/shard_map/psum | solution.py:234
  (115 other events, 1403.5 us)
Sparse Core Ops, SparseCore 0:
  9.9 39.6 all-gather.9
  52.6 27.9 all-gather.19
  82.7 27.4 all-gather.17
  112.2 36.5 all-gather.13
  150.8 35.9 all-gather.11
  239.3 21.0 all-reduce.16
  262.4 36.3 all-gather.21
  300.7 37.4 all-gather.15
  349.6 22.2 all-reduce.14
  409.9 45.0 reduce-scatter.42
  457.3 43.1 reduce-scatter.44
  502.7 59.5 reduce-scatter.30
  564.7 60.2 reduce-scatter.32
  629.2 30.3 all-reduce.12
  663.1 25.9 reduce-scatter.48
  691.9 35.1 reduce-scatter.50
  730.2 35.1 reduce-scatter.52
  768.8 28.5 reduce-scatter.36
  800.3 57.0 reduce-scatter.38
  860.3 57.0 reduce-scatter.40
  920.4 30.8 reduce-scatter.46
  954.4 47.2 reduce-scatter.34
  1005.2 26.0 reduce-scatter.64
  1034.6 28.5 reduce-scatter.58
  1066.5 24.0 reduce-scatter.60
  1094.1 24.4 reduce-scatter.54
  1122.0 24.0 reduce-scatter.62
  1149.4 24.4 reduce-scatter.56
  1176.8 187.2 all-reduce.10
